TPU v7x, 32 devices: a whole 2x2x4 slice. The times are simulated.
32 devices in a mesh: val: 4 (over x, core), cond: 8 (over z, y).
Axes of the slice: x: 2, y: 2, z: 4, core: 2. Of those that a mesh axis runs over, the one named last changes fastest.
Arguments:
- val_orbitals: bfloat16 [16, 768], P('val'), may hold values from -6 to 6
- cond_orbitals: bfloat16 [64, 768], P('cond'), may hold values from -6 to 6
- val_energy: bfloat16 [16], P('val'), may hold values from -0.59765625 to -0.049804688
- cond_energy: bfloat16 [64], P('cond'), may hold values from 0.049804688 to 1.1953125
- wave_index: int32 [4096], P('cond'), may hold values from 0 to 884735
Outputs:
- chi_real: float32 [128, 4096], P('val', 'cond')
- chi_imag: float32 [128, 4096], P('val', 'cond')
Inputs may be any that keep to these rules, and one draw needn't show every extreme that they name: `wave_index`: values may repeat.
All inputs are finite; a program needn't handle non-finite values.
Results may differ from a plain program's by a relative error of at most 0.0037.
Values may be sent and summed in bfloat16 or wider, within the bound.
A program may use at most 64 MiB of HBM per device.

v0:
```python
import math

import jax
import jax.numpy as jnp
from jax import lax
from jax.sharding import PartitionSpec as P

NG = 96
NW = 128
VB = 4
CB = 8
SLAB_Y = 4
NPTS = 768


def from_root(value, axis, source):
    kept = jnp.where(lax.axis_index(axis) == source, value, 0).astype(value.dtype)
    return lax.psum(kept, axis)


def phase_table(wave_index, point_count, grid_cells, slab_rows):
    points = lax.iota(jnp.int32, point_count)
    along_x = points % grid_cells
    along_y = points // grid_cells % slab_rows
    along_z = points // (grid_cells * slab_rows)
    wave_x = wave_index // (grid_cells * grid_cells)
    wave_y = wave_index // grid_cells % grid_cells
    wave_z = wave_index % grid_cells
    phase_turns = (
        along_x[:, None] * wave_x[None, :]
        + along_y[:, None] * wave_y[None, :]
        + along_z[:, None] * wave_z[None, :]
    ) % grid_cells
    angles = phase_turns.astype(jnp.float32) * (2.0 * math.pi / grid_cells)
    return jnp.concatenate([jnp.cos(angles), jnp.sin(angles)], axis=1).astype(jnp.bfloat16)


def pair_density(valence, conduction):
    product = conduction[:, None, :].astype(jnp.float32) * valence[None, :, :].astype(jnp.float32)
    return product.reshape(-1, valence.shape[1]).astype(jnp.bfloat16)


def pair_weights(val_energy, cond_energy):
    spread = cond_energy[:, None].astype(jnp.float32) - val_energy[None, :].astype(jnp.float32)
    return (1.0 / spread).reshape(-1)


def per_device(val_orbitals, cond_orbitals, val_energy, cond_energy, wave_index):
    window_index = from_root(wave_index[:NW], "cond", 0)
    row_table = phase_table(wave_index, NPTS, NG, SLAB_Y)
    window_table = phase_table(window_index, NPTS, NG, SLAB_Y)
    row_count = wave_index.shape[0]
    factor = -4.0 / math.sqrt(VB * lax.axis_size("val") * CB * lax.axis_size("cond"))
    conduction = lax.all_gather(cond_orbitals, "cond", axis=0, tiled=True)
    energy = lax.all_gather(cond_energy, "cond", axis=0, tiled=True)
    density = pair_density(val_orbitals, conduction)
    weights = pair_weights(val_energy, energy)
    window_terms = jnp.dot(density, window_table, preferred_element_type=jnp.float32)
    weighted = window_terms * weights[:, None]
    row_terms = jnp.dot(density, row_table, preferred_element_type=jnp.float32)
    update = jnp.dot(weighted.T, row_terms, precision=lax.Precision.HIGHEST)
    real_part = factor * (update[:NW, :row_count] + update[NW:, row_count:])
    imag_part = factor * (update[:NW, row_count:] - update[NW:, :row_count])
    return (
        lax.psum_scatter(real_part, "val", scatter_dimension=0, tiled=True),
        lax.psum_scatter(imag_part, "val", scatter_dimension=0, tiled=True),
    )


def solution(mesh):
    return jax.shard_map(
        per_device,
        mesh=mesh,
        in_specs=(P("val", None), P("cond", None), P("val"), P("cond"), P("cond")),
        out_specs=(P("val", "cond"), P("val", "cond")),
        check_vma=False,
    )
```

profile of v0, /device:TPU:0, one launch (start us, length us, event | category | flops | bytes accessed | tf_op | source)
XLA Modules:
  0.0 136.0 jit_solution(9349194043771805298)
XLA Ops:
  7.2 0.0 reduce-scatter.5.cloned.1.call-start
  7.3 0.7 add_select_fusion.9
  8.0 0.7 broadcast_select_fusion
  8.7 13.1 %psum.7 = s32[128]{0:T(128)S(1)} all-reduce(s32[128]{0:T(128)S(1)} %broadcast_select_fusion), channel_id=1, replica_groups=mesh['val'=4,'cond'=8] {'cond'}, use_global_device_ids=true, to_apply=%region_0.1 | all-reduce | flops 128 | bytes 1024 | tf_op jit(solution)/shard_map/psum | solution.py:18
  21.7 0.7 convert_element_type.36
  22.4 1.2 dynamic-slice
  24.3 0.9 dynamic-update-slice
  25.2 18.6 %all-reduce = bf16[64]{0:T(256)(128)(2,1)S(1)} all-reduce(bf16[64]{0:T(256)(128)(2,1)S(1)} %dynamic-update-slice), channel_id=1, replica_groups=mesh['val'=4,'cond'=8] {'cond'}, use_global_device_ids=true, to_apply=%add | all-reduce | flops 64 | bytes 256
  43.8 0.7 convert_element_type.31
  44.5 0.1 subtract_divide_fusion
  44.6 0.1 div.65
  44.7 30.8 %all_gather.6 = bf16[64,768]{1,0:T(8,128)(2,1)S(1)} all-gather(bf16[8,768]{1,0:T(8,128)(2,1)} %param.6), channel_id=1, replica_groups=mesh['val'=4,'cond'=8] {'cond'}, dimensions={0}, use_global_device_ids=true | all-gather | bytes 110592 | tf_op jit(solution)/shard_map/all_gather | solution.py:54
  75.5 0.1 multiply_convert_fusion
  75.6 0.1 convert_element_type.33
  75.7 2.4 %cosine_convert_fusion.1 = (bf16[768,128]{1,0:T(8,128)(2,1)S(1)}, bf16[768,128]{1,0:T(8,128)(2,1)S(1)}) fusion(s32[128]{0:T(128)S(1)} %get-tuple-element.13, s32[768]{0:T(1024)S(1)} %get-tuple-element.14, s32[128]{0:T(128)S(1)} %get-tuple-element.12, s32[768]{0:T(1024)S(1)} %get-tuple-element.15, s32[128]{0:T(128)S(1)} %get-tuple-element.11, ...), kind=kLoop, calls=%fused_computation.22 | loop fusion | flops 1474560 | bytes 403968 | tf_op jit(solution)/shard_map/convert.2
  78.1 7.6 %cosine_convert_fusion = (bf16[768,512]{1,0:T(8,128)(2,1)S(1)}, bf16[768,512]{1,0:T(8,128)(2,1)S(1)}) fusion(s32[512]{0:T(512)S(1)} %get-tuple-element.10, s32[768]{0:T(1024)S(1)} %get-tuple-element.14, s32[512]{0:T(512)S(1)} %get-tuple-element.9, s32[768]{0:T(1024)S(1)} %get-tuple-element.15, s32[512]{0:T(512)S(1)} %get-tuple-element.8, ...), kind=kLoop, calls=%fused_computation.8 | loop fusion | flops 5898240 | bytes 1588224 | tf_op jit(solution)/shard_map/convert
  85.7 0.6 fusion.2
  86.3 0.3 convolution_multiply_fusion
  86.6 1.0 fusion.31
  87.6 0.9 fusion.17
  88.5 0.0 reduce-scatter.5.cloned.1.call-update
  88.5 0.0 reduce-scatter.3.cloned.1.call-start
  88.6 0.7 reduce-scatter.3.cloned.1.call-update
  89.3 16.7 %reduce-scatter.5.cloned.1.call-done = f32[32,512]{1,0:T(8,128)} async-done(((f32[128,512]{1,0:T(8,128)}), f32[32,512]{1,0:T(8,128)}) %reduce-scatter.5.cloned.1.call-update) | async-done | bytes 65552 | tf_op jit(solution)/shard_map/reduce_scatter | solution.py:66
  106.0 23.1 %reduce-scatter.3.cloned.1.call-done = f32[32,512]{1,0:T(8,128)} async-done(((f32[128,512]{1,0:T(8,128)}), f32[32,512]{1,0:T(8,128)}) %reduce-scatter.3.cloned.1.call-update) | async-done | bytes 65552 | tf_op jit(solution)/shard_map/reduce_scatter | solution.py:65
  (6 shorter events, 0.1 us)
Async XLA Ops:
  7.2 98.8 %reduce-scatter.5.cloned.1.call-start = ((), (), s32[]{:S(2)}) async-start(), calls=%async_computation.3 | async-start | bytes 327680 | tf_op jit(solution)/shard_map/reduce_scatter | solution.py:66
  88.5 40.6 %reduce-scatter.3.cloned.1.call-start = ((), (), s32[]{:S(2)}) async-start(), calls=%async_computation.2 | async-start | bytes 327680 | tf_op jit(solution)/shard_map/reduce_scatter | solution.py:65
Sparse Core Ops, SparseCore 0:
  88.7 17.3 reduce-scatter.4
  109.0 20.0 reduce-scatter.2
where the time goes:
time: 136 us
  blocking collectives  62.5 us (46%)
  waiting for transfers between devices  40.6 us (30%)
  between operations  14.8 us (11%)
  other arithmetic  13.9 us (10%)
  local copies, waits for them, and re-layouts  2.3 us (2%)
  matrix products  1.87 us (1%)
    all_gather x1, blocking collectives, per_device(): conduction = lax.all_gather(cond_orbitals, 'cond', axis=0, tiled=True)  30.8 us
    reduce_scatter x1, waiting for transfers between devices, per_device(): lax.psum_scatter(real_part, 'val', scatter_dimension=0, tiled=True)  23.1 us
    unnamed x1, blocking collectives  18.6 us
    reduce_scatter x1, waiting for transfers between devices, per_device(): lax.psum_scatter(imag_part, 'val', scatter_dimension=0, tiled=True)  16.7 us
    psum x1, blocking collectives, from_root(): return lax.psum(kept, axis)  13.1 us
    another operation x2, other arithmetic  10 us
  transfers between devices with their start and end apart: 2, of which 2 were waited for; matrix products, arithmetic and copies ran while one was open for 0% of the time, Pallas kernels for 0%

commit v1 on v0

v1 whole, which is shorter than its diff:
```python
import functools
import math

import jax
import jax.numpy as jnp
from jax import lax
from jax.experimental import pallas as pl
from jax.experimental.pallas import tpu as pltpu
from jax.sharding import PartitionSpec as P

NG = 96
NW = 128
SLAB_Y = 4
LANES = 128
MESH = pl.DeviceIdType.MESH


def modulo(value, period):
    return value - period * jnp.floor((value + 0.5) * (1.0 / period))


def cos_turns(turns):
    angle = (turns - NG / 2) * (math.pi / NG)
    square = angle * angle
    series = 1.0
    for order in (10, 8, 6, 4, 2):
        series = 1.0 - square * series * (1.0 / (order * (order + 1)))
    sine = angle * series
    return 2.0 * sine * sine - 1.0


def wave_parts(index):
    flat = index.astype(jnp.float32)
    wave_x = jnp.floor((flat + 0.5) * (1.0 / (NG * NG)))
    rest = flat - wave_x * (NG * NG)
    wave_y = jnp.floor((rest + 0.5) * (1.0 / NG))
    return wave_x, wave_y, rest - wave_y * NG


def factors(index, points, shift):
    wave_x, wave_y, wave_z = wave_parts(index)
    planes = points // NG
    along_x = lax.broadcasted_iota(jnp.int32, (NG, LANES), 0).astype(jnp.float32)
    plane = lax.broadcasted_iota(jnp.int32, (planes, LANES), 0).astype(jnp.float32)
    along_z = jnp.floor((plane + 0.5) * (1.0 / SLAB_Y))
    along_y = plane - along_z * SLAB_Y
    turns_x = modulo(along_x * wave_x, NG)
    turns_yz = modulo(along_y * wave_y + along_z * wave_z + shift, NG)
    quarter = 3 * NG // 4
    return (
        cos_turns(turns_x),
        cos_turns(modulo(turns_x + quarter, NG)),
        cos_turns(turns_yz),
        cos_turns(modulo(turns_yz + quarter, NG)),
    )


def split(value):
    high = value.astype(jnp.bfloat16)
    low = (value - high.astype(jnp.float32)).astype(jnp.bfloat16)
    return jnp.concatenate([high, low], axis=0)


def dot(left, right):
    return jnp.dot(left, right, preferred_element_type=jnp.float32)


def kernel(
    nv, nc, vb, cb, points,
    packed, wave, real, imag,
    gath_v, gath_c, own_wave, window, cos_rows, sin_rows, window_table, dens, totals,
    send_v, recv_v, send_c, recv_c, send_w, recv_w, local,
):
    iv = lax.axis_index("val")
    ic = lax.axis_index("cond")
    rows = NW // nv
    planes = points // NG

    barrier = pltpu.get_barrier_semaphore()
    for d in range(1, nc):
        pl.semaphore_signal(barrier, inc=1, device_id={"cond": lax.rem(ic + d, nc)}, device_id_type=MESH)
    for d in range(1, nv):
        pl.semaphore_signal(barrier, inc=1, device_id={"val": lax.rem(iv + d, nv)}, device_id_type=MESH)

    wave_copy = pltpu.make_async_copy(wave, own_wave, local.at[0])
    cond_copy = pltpu.make_async_copy(packed.at[0], gath_c.at[ic], local.at[1])
    val_copy = pltpu.make_async_copy(packed.at[1], gath_v.at[iv], local.at[2])
    wave_copy.start()
    cond_copy.start()
    val_copy.start()
    wave_copy.wait()

    for block in range(own_wave.shape[0]):
        cos_x, sin_x, cos_p, sin_p = factors(own_wave[pl.ds(block, 1), :], points, 0.0)
        lanes = pl.ds(block * LANES, LANES)
        for plane in range(planes):
            at = pl.ds(plane * NG, NG)
            c, s = cos_p[plane:plane + 1, :], sin_p[plane:plane + 1, :]
            cos_rows[at, lanes] = (cos_x * c - sin_x * s).astype(jnp.bfloat16)
            sin_rows[at, lanes] = (sin_x * c + cos_x * s).astype(jnp.bfloat16)

    pl.semaphore_wait(barrier, nc - 1 + nv - 1)

    def window_copy(d):
        return pltpu.make_async_remote_copy(
            src_ref=wave.at[pl.ds(0, 1)], dst_ref=window,
            send_sem=send_w.at[d - 1], recv_sem=recv_w,
            device_id={"cond": lax.rem(ic + d, nc)}, device_id_type=MESH,
        )

    @pl.when(ic == 0)
    def _():
        for d in range(1, nc):
            window_copy(d).start()
        pltpu.make_async_copy(wave.at[pl.ds(0, 1)], window, local.at[3]).start()

    def cond_send(d):
        return pltpu.make_async_remote_copy(
            src_ref=packed.at[0], dst_ref=gath_c.at[ic],
            send_sem=send_c.at[d - 1], recv_sem=recv_c.at[d - 1],
            device_id={"cond": lax.rem(ic + d, nc)}, device_id_type=MESH,
        )

    def cond_recv(d):
        return pltpu.make_async_remote_copy(
            src_ref=packed.at[0], dst_ref=gath_c.at[lax.rem(ic + nc - d, nc)],
            send_sem=send_c.at[d - 1], recv_sem=recv_c.at[d - 1],
            device_id={"cond": lax.rem(ic + d, nc)}, device_id_type=MESH,
        )

    def val_send(d):
        return pltpu.make_async_remote_copy(
            src_ref=packed.at[1], dst_ref=gath_v.at[iv],
            send_sem=send_v.at[d - 1], recv_sem=recv_v.at[d - 1],
            device_id={"val": lax.rem(iv + d, nv)}, device_id_type=MESH,
        )

    def val_recv(d):
        return pltpu.make_async_remote_copy(
            src_ref=packed.at[1], dst_ref=gath_v.at[lax.rem(iv + nv - d, nv)],
            send_sem=send_v.at[d - 1], recv_sem=recv_v.at[d - 1],
            device_id={"val": lax.rem(iv + d, nv)}, device_id_type=MESH,
        )

    for d in range(1, nc):
        cond_send(d).start()
    for d in range(1, nv):
        val_send(d).start()

    @pl.when(ic == 0)
    def _():
        pltpu.make_async_copy(wave.at[pl.ds(0, 1)], window, local.at[3]).wait()

    @pl.when(ic != 0)
    def _():
        window_copy(1).wait_recv()

    spread = jnp.broadcast_to(window[...], (8, LANES))
    first = pltpu.roll(spread, lax.rem(NW - iv * rows, NW), 1)
    lane = lax.broadcasted_iota(jnp.int32, (8, LANES), 1)
    index = jnp.where(lane < rows, first, pltpu.roll(first, rows, 1))[0:1, :]
    shift = jnp.where(lane < rows, 0.0, 3 * NG / 4)[0:1, :]
    cos_x, sin_x, cos_p, sin_p = factors(index, points, shift)
    for plane in range(planes):
        c, s = cos_p[plane:plane + 1, :], sin_p[plane:plane + 1, :]
        window_table[pl.ds(plane * NG, NG), :] = (cos_x * c - sin_x * s).astype(jnp.bfloat16)

    val_copy.wait()
    cond_copy.wait()
    for d in range(1, nv):
        val_recv(d).wait_recv()
    for d in range(1, nc):
        cond_recv(d).wait_recv()

    count = nc * cb
    per_step = max(1, min(nv, 1024 // (count * vb)))
    totals[...] = jnp.zeros_like(totals)

    @pl.loop(0, nv // per_step)
    def _(step):
        cond = gath_c[:, 0:cb, 0:points].astype(jnp.float32).reshape(count, points)
        cond_energy = gath_c[:, 0:cb, points:points + LANES].astype(jnp.float32).reshape(count, LANES)
        weights = []
        for inner in range(per_step):
            block = gath_v[step * per_step + inner].astype(jnp.float32)
            for v in range(vb):
                at = pl.ds((inner * vb + v) * count, count)
                dens[at, :] = (cond * block[v:v + 1, 0:points]).astype(jnp.bfloat16)
                weights.append(1.0 / (cond_energy - block[v:v + 1, points:points + LANES]))
        weighted = dot(dens[...], window_table[...]) * jnp.concatenate(weights, axis=0)
        parts = split(jnp.transpose(weighted)[0:2 * rows])
        update = dot(parts, dens[...])
        totals[...] += update[0:2 * rows] + update[2 * rows:4 * rows]

    cos_total = totals[0:rows, :]
    sin_total = totals[rows:2 * rows, :]
    by_cos = split(jnp.concatenate([cos_total, -sin_total], axis=0))
    by_sin = split(jnp.concatenate([sin_total, cos_total], axis=0))
    both = dot(by_cos, cos_rows[...]) + dot(by_sin, sin_rows[...])
    factor = -4.0 / math.sqrt(nv * vb * count)
    both = factor * (both[0:2 * rows] + both[2 * rows:4 * rows])
    real[...] = both[0:rows]
    imag[...] = both[rows:2 * rows]

    @pl.when(ic == 0)
    def _():
        for d in range(1, nc):
            window_copy(d).wait_send()

    for d in range(1, nc):
        cond_send(d).wait_send()
    for d in range(1, nv):
        val_send(d).wait_send()


def per_device(val_orbitals, cond_orbitals, val_energy, cond_energy, wave_index):
    nv, nc = lax.axis_size("val"), lax.axis_size("cond")
    vb, points = val_orbitals.shape
    cb = cond_orbitals.shape[0]
    held = -(-max(vb, cb) // 8) * 8
    count = wave_index.shape[0]
    rows = NW // nv

    def pack(orbitals, energy):
        wide = jnp.broadcast_to(energy[:, None], (energy.shape[0], LANES))
        both = jnp.concatenate([orbitals, wide], axis=1)
        return jnp.pad(both, ((0, held - both.shape[0]), (0, 0)))

    packed = jnp.stack([pack(cond_orbitals, cond_energy), pack(val_orbitals, val_energy)])
    wave = wave_index.reshape(count // LANES, LANES)
    width = points + LANES
    pairs = max(1, min(nv, 1024 // (nc * cb * vb))) * vb * nc * cb
    shape = jax.ShapeDtypeStruct((rows, count), jnp.float32)
    return pl.pallas_call(
        functools.partial(kernel, nv, nc, vb, cb, points),
        out_shape=(shape, shape),
        in_specs=[pl.BlockSpec(memory_space=pl.ANY)] * 2,
        out_specs=[pl.BlockSpec(memory_space=pltpu.VMEM)] * 2,
        scratch_shapes=[
            pltpu.VMEM((nv, held, width), jnp.bfloat16),
            pltpu.VMEM((nc, held, width), jnp.bfloat16),
            pltpu.VMEM((count // LANES, LANES), jnp.int32),
            pltpu.VMEM((1, LANES), jnp.int32),
            pltpu.VMEM((points, count), jnp.bfloat16),
            pltpu.VMEM((points, count), jnp.bfloat16),
            pltpu.VMEM((points, LANES), jnp.bfloat16),
            pltpu.VMEM((pairs, points), jnp.bfloat16),
            pltpu.VMEM((2 * rows, points), jnp.float32),
            pltpu.SemaphoreType.DMA((nv - 1,)),
            pltpu.SemaphoreType.DMA((nv - 1,)),
            pltpu.SemaphoreType.DMA((nc - 1,)),
            pltpu.SemaphoreType.DMA((nc - 1,)),
            pltpu.SemaphoreType.DMA((nc - 1,)),
            pltpu.SemaphoreType.DMA,
            pltpu.SemaphoreType.DMA((4,)),
        ],
        compiler_params=pltpu.CompilerParams(collective_id=0, has_side_effects=True),
    )(packed, wave)


def solution(mesh):
    return jax.shard_map(
        per_device,
        mesh=mesh,
        in_specs=(P("val", None), P("cond", None), P("val"), P("cond"), P("cond")),
        out_specs=(P("val", "cond"), P("val", "cond")),
        check_vma=False,
    )
```

time: 136 us -> 18.5 us (0.14)
  blocking collectives: 62.5 us -> 0 us
  waiting for transfers between devices: 40.6 us -> 0 us
  between operations: 14.8 us -> 0.66 us
  Pallas kernels: 0 us -> 12.6 us
  other arithmetic: 13.9 us -> 1.33 us
  matrix products: 1.87 us -> 0 us
    reduce_scatter x2 -> x0, waiting for transfers between devices: 39.8 us -> none  [the longest x1 23.1 us: per_device(): lax.psum_scatter(real_part, 'val', scatter_dimension=0, tiled=True)]
    all_gather x1 -> x0, blocking collectives: 30.8 us -> none  [per_device(): conduction = lax.all_gather(cond_orbitals, 'cond', axis=0, tiled=True)]
    unnamed x1 -> x0, blocking collectives: 18.6 us -> none
    psum x1 -> x0, blocking collectives: 13.1 us -> none  [from_root(): return lax.psum(kept, axis)]
    pallas_call x0 -> x1, Pallas kernels: none -> 12.6 us  [per_device(): pl.pallas_call(functools.partial(kernel, nv, nc, vb, cb, points), out_sha...]
    another operation x2, other arithmetic: 10 us -> 1.33 us  [per_device(): jnp.stack([pack(cond_orbitals, cond_energy), pack(val_orbitals, val_energ...]
    dot_general x3 -> x0, matrix products: 1.87 us -> none  [the longest x1 1.03 us: per_device(): update = jnp.dot(weighted.T, row_terms, precision=lax.Precision.HIGHEST)]
    convert_element_type x5 -> x0, other arithmetic: 1.51 us -> none  [the longest x1 0.7 us: pair_density(): valence[None, :, :].astype(jnp.float32)]
  transfers between devices with their start and end apart: 2 -> 0, of which waited for: 2 -> 0; matrix products, arithmetic and copies ran while one was open for 0% -> 0% of each run, Pallas kernels for 0% -> 0%
where the time goes in v1:
time: 18.5 us; the launch traced here: 18.2 us
  Pallas kernels  12.6 us (68%)
  local copies, waits for them, and re-layouts  3.6 us (19%)
  other arithmetic  1.33 us (7%)
  between operations  0.66 us (4%)
    pallas_call x1, Pallas kernels, per_device(): pl.pallas_call(functools.partial(kernel, nv, nc, vb, cb, points), out_sha...  12.6 us
    unnamed x6, local copies, waits for them, and re-layouts  2.14 us
    broadcast_in_dim x2, local copies, waits for them, and re-layouts, pack(): wide = jnp.broadcast_to(energy[:, None], (energy.shape[0], LANES))  1.46 us
    another operation x2, other arithmetic, per_device(): jnp.stack([pack(cond_orbitals, cond_energy), pack(val_orbitals, val_energ...  1.33 us

profile of v1, /device:TPU:0, one launch (start us, length us, event | category | flops | bytes accessed | tf_op | source)
XLA Modules:
  0.0 18.2 jit_solution(6892369779481249879)
XLA Ops:
  0.6 0.0 copy-start.1
  0.6 0.7 %broadcast_in_dim.5 = bf16[4,128]{1,0:T(4,128)(2,1)S(1)} broadcast(bf16[4]{0:T(256)(128)(2,1)} %param.7), dimensions={0} | broadcast | bytes 1032 | tf_op jit(solution)/shard_map/broadcast_in_dim | solution.py:225
  1.4 0.7 %broadcast_in_dim.4 = bf16[8,128]{1,0:T(8,128)(2,1)S(1)} broadcast(bf16[8]{0:T(256)(128)(2,1)} %param.8), dimensions={0} | broadcast | bytes 2064 | tf_op jit(solution)/shard_map/broadcast_in_dim | solution.py:225
  2.1 0.0 copy-done.1
  2.1 0.7 %fusion.3 = (bf16[1,8,896]{2,1,0:T(8,128)(2,1)S(1)}, bf16[1,8,896]{2,1,0:T(8,128)(2,1)S(1)}) fusion(bf16[4,128]{1,0:T(4,128)(2,1)S(1)} %broadcast_in_dim.5, bf16[4,768]{1,0:T(4,128)(2,1)S(1)} %copy-done.1, bf16[8,128]{1,0:T(8,128)(2,1)S(1)} %broadcast_in_dim.4, bf16[8,768]{1,0:T(8,128)(2,1)} %param.6), kind=kLoop, calls=%fused_computation.5 | loop fusion | flops 78848 | bytes 50176 | tf_op jit(solution)/shard_map/stack | solution.py:229
  2.8 0.6 %pad_maximum_fusion.packed = bf16[2,8,896]{2,1,0:T(8,128)(2,1)} fusion(bf16[1,8,896]{2,1,0:T(8,128)(2,1)S(1)} %get-tuple-element.2, bf16[1,8,896]{2,1,0:T(8,128)(2,1)S(1)} %get-tuple-element.3), kind=kLoop, calls=%fused_computation.3 | loop fusion | flops 14336 | bytes 57344 | tf_op jit(solution)/shard_map/stack | solution.py:229
  3.4 12.6 %shard_map.68 = (f32[32,512]{1,0:T(8,128)}, f32[32,512]{1,0:T(8,128)}) custom-call(bf16[2,8,896]{2,1,0:T(8,128)(2,1)} %pad_maximum_fusion.packed, s32[4,128]{1,0:T(4,128)} %bitcast.5), custom_call_target="tpu_custom_call" | custom-call | tf_op jit(solution)/shard_map/pallas_call | solution.py:234
  16.1 0.0 copy-start
  16.1 1.5 %copy.9 = f32[32,512]{1,0:T(8,128)} copy(f32[32,512]{1,0:T(8,128)} %get-tuple-element.6) | data formatting | bytes 131072
  17.6 0.0 copy-done
  17.6 0.6 %copy.10 = f32[32,512]{1,0:T(8,128)} copy(f32[32,512]{1,0:T(8,128)S(1)} %copy-done) | data formatting | bytes 131072
Async XLA Ops:
  0.6 1.5 %copy-start.1 = (bf16[4,768]{1,0:T(4,128)(2,1)S(1)}, bf16[4,768]{1,0:T(4,128)(2,1)}, u32[]{:S(2)}) copy-start(bf16[4,768]{1,0:T(4,128)(2,1)} %param.5) | copy-start | bytes 18436
  16.1 1.5 %copy-start = (f32[32,512]{1,0:T(8,128)S(1)}, f32[32,512]{1,0:T(8,128)}, u32[]{:S(2)}) copy-start(f32[32,512]{1,0:T(8,128)} %get-tuple-element.7) | copy-start | bytes 196612

commit v2 on v1

v2 whole, which is shorter than its diff:
```python
import functools
import math

import jax
import jax.numpy as jnp
from jax import lax
from jax.experimental import pallas as pl
from jax.experimental.pallas import tpu as pltpu
from jax.sharding import PartitionSpec as P

NG = 96
NW = 128
SLAB_Y = 4
LANES = 128
VMEM_LIMIT = 24 * 1024 * 1024
MESH = pl.DeviceIdType.MESH


def modulo(value, period):
    return value - period * jnp.floor((value + 0.5) * (1.0 / period))


def cos_turns(turns):
    angle = (turns - NG / 2) * (math.pi / NG)
    square = angle * angle
    series = 1.0
    for order in (10, 8, 6, 4, 2):
        series = 1.0 - square * series * (1.0 / (order * (order + 1)))
    sine = angle * series
    return 2.0 * sine * sine - 1.0


def wave_parts(index):
    flat = index.astype(jnp.float32)
    wave_x = jnp.floor((flat + 0.5) * (1.0 / (NG * NG)))
    rest = flat - wave_x * (NG * NG)
    wave_y = jnp.floor((rest + 0.5) * (1.0 / NG))
    return wave_x, wave_y, rest - wave_y * NG


def factors(index, points, shift):
    wave_x, wave_y, wave_z = wave_parts(index)
    planes = points // NG
    along_x = lax.broadcasted_iota(jnp.int32, (NG, LANES), 0).astype(jnp.float32)
    plane = lax.broadcasted_iota(jnp.int32, (planes, LANES), 0).astype(jnp.float32)
    along_z = jnp.floor((plane + 0.5) * (1.0 / SLAB_Y))
    along_y = plane - along_z * SLAB_Y
    turns_x = modulo(along_x * wave_x, NG)
    turns_yz = modulo(along_y * wave_y + along_z * wave_z + shift, NG)
    quarter = 3 * NG // 4
    return (
        cos_turns(turns_x),
        cos_turns(modulo(turns_x + quarter, NG)),
        cos_turns(turns_yz),
        cos_turns(modulo(turns_yz + quarter, NG)),
    )


def split(value):
    high = value.astype(jnp.bfloat16)
    low = (value - high.astype(jnp.float32)).astype(jnp.bfloat16)
    return jnp.concatenate([high, low], axis=0)


def dot(left, right):
    return jnp.dot(left, right, preferred_element_type=jnp.float32)


def partner(position, offset, size):
    if size & (size - 1):
        return lax.rem(position + offset, size)
    bit = 1
    while bit < size:
        if offset & bit:
            position = position + bit - 2 * bit * lax.rem(position // bit, 2)
        bit *= 2
    return position


def source(position, offset, size):
    if size & (size - 1):
        return lax.rem(position + size - offset, size)
    return partner(position, offset, size)


def kernel(
    nv, nc, group, slots,
    val, cond, val_energy, cond_energy, wave, out,
    gath_v, gath_c, gath_ve, gath_ce, own_wave, window, cos_rows, sin_rows, window_table, dens, totals,
    send_v, recv_v, send_c, recv_c, send_ve, recv_ve, send_ce, recv_ce, send_w, recv_w, local,
):
    iv = lax.axis_index("val")
    ic = lax.axis_index("cond")
    vb, points = val.shape
    cb = cond.shape[0]
    rows = NW // nv
    planes = points // NG

    barrier = pltpu.get_barrier_semaphore()
    for d in range(nc - 1, 0, -1):
        pl.semaphore_signal(barrier, inc=1, device_id={"cond": partner(ic, d, nc)}, device_id_type=MESH)
    for d in range(1, nv):
        pl.semaphore_signal(barrier, inc=1, device_id={"val": partner(iv, d, nv)}, device_id_type=MESH)

    wave_copy = pltpu.make_async_copy(wave, own_wave, local.at[0])
    own_copies = [
        pltpu.make_async_copy(val, gath_v.at[iv], local.at[1]),
        pltpu.make_async_copy(val_energy, gath_ve.at[iv], local.at[2]),
        pltpu.make_async_copy(cond, gath_c.at[ic], local.at[3]),
        pltpu.make_async_copy(cond_energy, gath_ce.at[ic], local.at[4]),
    ]
    wave_copy.start()
    for copy in own_copies:
        copy.start()
    wave_copy.wait()

    for block in range(own_wave.shape[0]):
        cos_x, sin_x, cos_p, sin_p = factors(own_wave[pl.ds(block, 1), :], points, 0.0)
        lanes = pl.ds(block * LANES, LANES)
        for plane in range(planes):
            at = pl.ds(plane * NG, NG)
            c, s = cos_p[plane:plane + 1, :], sin_p[plane:plane + 1, :]
            cos_rows[at, lanes] = (cos_x * c - sin_x * s).astype(jnp.bfloat16)
            sin_rows[at, lanes] = (sin_x * c + cos_x * s).astype(jnp.bfloat16)

    pl.semaphore_wait(barrier, nc - 1 + nv - 1)

    def window_copy(d):
        return pltpu.make_async_remote_copy(
            src_ref=wave.at[pl.ds(0, 1)], dst_ref=window,
            send_sem=send_w.at[d - 1], recv_sem=recv_w,
            device_id={"cond": partner(ic, d, nc)}, device_id_type=MESH,
        )

    own_window = pltpu.make_async_copy(wave.at[pl.ds(0, 1)], window, local.at[5])

    @pl.when(ic == 0)
    def _():
        for d in range(nc - 1, 0, -1):
            window_copy(d).start()
        own_window.start()

    def exchange(axis, position, size, d, at, src, dst, send, recv):
        return pltpu.make_async_remote_copy(
            src_ref=src, dst_ref=dst.at[at],
            send_sem=send.at[d - 1], recv_sem=recv.at[d - 1],
            device_id={axis: partner(position, d, size)}, device_id_type=MESH,
        )

    def val_copies(d, at):
        return [
            exchange("val", iv, nv, d, at, val, gath_v, send_v, recv_v),
            exchange("val", iv, nv, d, at, val_energy, gath_ve, send_ve, recv_ve),
        ]

    def cond_copies(d, at):
        return [
            exchange("cond", ic, nc, d, at, cond, gath_c, send_c, recv_c),
            exchange("cond", ic, nc, d, at, cond_energy, gath_ce, send_ce, recv_ce),
        ]

    for d in range(nc - 1, 0, -1):
        for copy in cond_copies(d, ic):
            copy.start()
    for d in range(1, nv):
        for copy in val_copies(d, iv):
            copy.start()

    for copy in own_copies:
        copy.wait()
    for d in range(1, nv):
        for copy in val_copies(d, source(iv, d, nv)):
            copy.wait_recv()

    count = group * cb
    height = nv * vb * count
    eye = lax.broadcasted_iota(jnp.int32, (cb, cb), 0) == lax.broadcasted_iota(jnp.int32, (cb, cb), 1)

    def fill(first):
        slot = first // group % slots
        orbitals, energies = [], []
        for d in range(first, first + group):
            at = source(ic, d, nc) if d else ic
            if d:
                for copy in cond_copies(d, at):
                    copy.wait_recv()
            orbitals.append(gath_c[at].astype(jnp.float32))
            row = jnp.broadcast_to(gath_ce[at].astype(jnp.float32), (cb, cb))
            column = jnp.sum(jnp.where(eye, row, 0.0), axis=1, keepdims=True)
            energies.append(jnp.broadcast_to(column, (cb, LANES)))
        orbitals = jnp.concatenate(orbitals, axis=0)

        def one_block(b, carry):
            block = gath_v[b].astype(jnp.float32)
            for v in range(vb):
                at = pl.ds(pl.multiple_of((b * vb + v) * count, count), count)
                dens[slot, at, :] = (orbitals * block[v:v + 1, :]).astype(jnp.bfloat16)
            return carry

        lax.fori_loop(0, nv, one_block, 0, unroll=nv <= 4)
        return jnp.concatenate(energies, axis=0)

    def use(first, energies):
        slot = first // group % slots
        weights = []
        for b in range(nv):
            block = gath_ve[b].astype(jnp.float32)
            for v in range(vb):
                own = jnp.broadcast_to(block[:, v:v + 1], (1, LANES))
                weights.append(1.0 / (energies - own))
        weighted = dot(dens[slot], window_table[...]) * jnp.concatenate(weights, axis=0)
        update = dot(split(jnp.transpose(weighted)[0:2 * rows]), dens[slot])
        update = update[0:2 * rows] + update[2 * rows:4 * rows]
        totals[...] = update if first == 0 else totals[...] + update

    ahead = min(2, slots, nc // group)
    energies = {}
    for step in range(ahead):
        energies[step] = fill(step * group)

    @pl.when(ic == 0)
    def _():
        own_window.wait()

    @pl.when(ic != 0)
    def _():
        window_copy(1).wait_recv()

    spread = jnp.broadcast_to(window[...], (8, LANES))
    first = pltpu.roll(spread, lax.rem(NW - iv * rows, NW), 1)
    lane = lax.broadcasted_iota(jnp.int32, (8, LANES), 1)
    index = jnp.where(lane < rows, first, pltpu.roll(first, rows, 1))[0:1, :]
    shift = jnp.where(lane < rows, 0.0, 3 * NG / 4)[0:1, :]
    cos_x, sin_x, cos_p, sin_p = factors(index, points, shift)
    for plane in range(planes):
        c, s = cos_p[plane:plane + 1, :], sin_p[plane:plane + 1, :]
        window_table[pl.ds(plane * NG, NG), :] = (cos_x * c - sin_x * s).astype(jnp.bfloat16)

    for step in range(nc // group):
        if step >= ahead:
            energies[step] = fill(step * group)
        use(step * group, energies.pop(step))

    cos_total = totals[0:rows, :]
    sin_total = totals[rows:2 * rows, :]
    by_cos = split(jnp.concatenate([cos_total, -sin_total], axis=0))
    by_sin = split(jnp.concatenate([sin_total, cos_total], axis=0))
    both = dot(by_cos, cos_rows[...]) + dot(by_sin, sin_rows[...])
    out[...] = both[0:2 * rows] + both[2 * rows:4 * rows]

    @pl.when(ic == 0)
    def _():
        for d in range(1, nc):
            window_copy(d).wait_send()

    for d in range(1, nc):
        for copy in cond_copies(d, ic):
            copy.wait_send()
    for d in range(1, nv):
        for copy in val_copies(d, iv):
            copy.wait_send()


def per_device(val_orbitals, cond_orbitals, val_energy, cond_energy, wave_index):
    nv, nc = lax.axis_size("val"), lax.axis_size("cond")
    vb, points = val_orbitals.shape
    cb = cond_orbitals.shape[0]
    count = wave_index.shape[0]
    rows = NW // nv
    group = 2 if nc % 2 == 0 else 1
    slots = min(4, nc // group)
    bf16, f32 = jnp.bfloat16, jnp.float32
    dma = pltpu.SemaphoreType.DMA
    out = pl.pallas_call(
        functools.partial(kernel, nv, nc, group, slots),
        out_shape=jax.ShapeDtypeStruct((2 * rows, count), f32),
        in_specs=[pl.BlockSpec(memory_space=pltpu.HBM)] * 5,
        out_specs=pl.BlockSpec(memory_space=pltpu.VMEM),
        scratch_shapes=[
            pltpu.VMEM((nv, vb, points), bf16),
            pltpu.VMEM((nc, cb, points), bf16),
            pltpu.VMEM((nv, 1, vb), bf16),
            pltpu.VMEM((nc, 1, cb), bf16),
            pltpu.VMEM((count // LANES, LANES), jnp.int32),
            pltpu.VMEM((1, LANES), jnp.int32),
            pltpu.VMEM((points, count), bf16),
            pltpu.VMEM((points, count), bf16),
            pltpu.VMEM((points, LANES), bf16),
            pltpu.VMEM((slots, nv * vb * group * cb, points), bf16),
            pltpu.VMEM((2 * rows, points), f32),
            dma((nv - 1,)), dma((nv - 1,)), dma((nc - 1,)), dma((nc - 1,)),
            dma((nv - 1,)), dma((nv - 1,)), dma((nc - 1,)), dma((nc - 1,)),
            dma((nc - 1,)), dma, dma((6,)),
        ],
        compiler_params=pltpu.CompilerParams(
            collective_id=0, has_side_effects=True, vmem_limit_bytes=VMEM_LIMIT
        ),
    )(*[
        pltpu.with_memory_space_constraint(value, pltpu.HBM)
        for value in (
            val_orbitals, cond_orbitals, val_energy.reshape(1, vb), cond_energy.reshape(1, cb),
            wave_index.reshape(count // LANES, LANES),
        )
    ])
    factor = -4.0 / math.sqrt(nv * vb * nc * cb)
    return factor * out[0:rows], factor * out[rows:2 * rows]


def solution(mesh):
    return jax.shard_map(
        per_device,
        mesh=mesh,
        in_specs=(P("val", None), P("cond", None), P("val"), P("cond"), P("cond")),
        out_specs=(P("val", "cond"), P("val", "cond")),
        check_vma=False,
    )
```

time: 18.5 us -> 14.4 us (0.78)
  local copies, waits for them, and re-layouts: 3.6 us -> 0 us
  other arithmetic: 1.33 us -> 0.66 us
  Pallas kernels: 12.6 us -> 12.9 us
    unnamed x6 -> x0, local copies, waits for them, and re-layouts: 2.14 us -> none
    broadcast_in_dim x2 -> x0, local copies, waits for them, and re-layouts: 1.46 us -> none  [pack(): wide = jnp.broadcast_to(energy[:, None], (energy.shape[0], LANES))]
    another operation x2 -> x0, other arithmetic: 1.33 us -> none  [per_device(): jnp.stack([pack(cond_orbitals, cond_energy), pack(val_orbitals, val_energ...]
    mul x0 -> x1, other arithmetic: none -> 0.66 us  [per_device(): return (factor * out[0:rows], factor * out[rows:2 * rows])]
    pallas_call x1, Pallas kernels: 12.6 us -> 12.9 us  [per_device(): pl.pallas_call(functools.partial(kernel, nv, nc, group, slots), out_shape...]
where the time goes in v2:
time: 14.4 us; the launch traced here: 14.2 us
  Pallas kernels  12.9 us (90%)
  other arithmetic  0.66 us (5%)
  between operations  0.64 us (4%)
    pallas_call x1, Pallas kernels, per_device(): pl.pallas_call(functools.partial(kernel, nv, nc, group, slots), out_shape...  12.9 us
    mul x1, other arithmetic, per_device(): return (factor * out[0:rows], factor * out[rows:2 * rows])  0.66 us

profile of v2, /device:TPU:0, one launch (start us, length us, event | category | flops | bytes accessed | tf_op | source)
XLA Modules:
  0.0 14.2 jit_solution(6719474297901607500)
XLA Ops:
  0.6 12.9 %shard_map.68 = f32[64,512]{1,0:T(8,128)S(1)} custom-call(bf16[4,768]{1,0:T(4,128)(2,1)} %val.1, bf16[8,768]{1,0:T(8,128)(2,1)} %cond.1, bf16[1,4]{1,0:T(2,128)(2,1)} %bitcast.4, bf16[1,8]{1,0:T(2,128)(2,1)} %bitcast.5, s32[4,128]{1,0:T(4,128)} %bitcast.3), custom_call_target="tpu_custom_call" | custom-call | tf_op jit(solution)/shard_map/pallas_call | solution.py:274
  13.6 0.7 %slice_multiply_fusion = (f32[32,512]{1,0:T(8,128)}, f32[32,512]{1,0:T(8,128)}) fusion(f32[64,512]{1,0:T(8,128)S(1)} %shard_map.68), kind=kLoop, calls=%fused_computation | loop fusion | flops 32768 | bytes 262144 | tf_op jit(solution)/shard_map/mul | solution.py:306

commit v3 on v2

--- a/solution.py
+++ b/solution.py
@@ -112,6 +112,49 @@
     wave_copy.start()
     for copy in own_copies:
         copy.start()
+    pl.semaphore_wait(barrier, nc - 1 + nv - 1)
+
+    def window_copy(d):
+        return pltpu.make_async_remote_copy(
+            src_ref=wave.at[pl.ds(0, 1)], dst_ref=window,
+            send_sem=send_w.at[d - 1], recv_sem=recv_w,
+            device_id={"cond": partner(ic, d, nc)}, device_id_type=MESH,
+        )
+
+    own_window = pltpu.make_async_copy(wave.at[pl.ds(0, 1)], window, local.at[5])
+
+    @pl.when(ic == 0)
+    def _():
+        for d in range(nc - 1, 0, -1):
+            window_copy(d).start()
+        own_window.start()
+
+    def exchange(axis, position, size, d, at, src, dst, send, recv):
+        return pltpu.make_async_remote_copy(
+            src_ref=src, dst_ref=dst.at[at],
+            send_sem=send.at[d - 1], recv_sem=recv.at[d - 1],
+            device_id={axis: partner(position, d, size)}, device_id_type=MESH,
+        )
+
+    def val_copies(d, at):
+        return [
+            exchange("val", iv, nv, d, at, val, gath_v, send_v, recv_v),
+            exchange("val", iv, nv, d, at, val_energy, gath_ve, send_ve, recv_ve),
+        ]
+
+    def cond_copies(d, at):
+        return [
+            exchange("cond", ic, nc, d, at, cond, gath_c, send_c, recv_c),
+            exchange("cond", ic, nc, d, at, cond_energy, gath_ce, send_ce, recv_ce),
+        ]
+
+    for d in range(nc - 1, 0, -1):
+        for copy in cond_copies(d, ic):
+            copy.start()
+    for d in range(1, nv):
+        for copy in val_copies(d, iv):
+            copy.start()
+
     wave_copy.wait()
 
     for block in range(own_wave.shape[0]):
@@ -122,49 +165,6 @@
             c, s = cos_p[plane:plane + 1, :], sin_p[plane:plane + 1, :]
             cos_rows[at, lanes] = (cos_x * c - sin_x * s).astype(jnp.bfloat16)
             sin_rows[at, lanes] = (sin_x * c + cos_x * s).astype(jnp.bfloat16)
-
-    pl.semaphore_wait(barrier, nc - 1 + nv - 1)
-
-    def window_copy(d):
-        return pltpu.make_async_remote_copy(
-            src_ref=wave.at[pl.ds(0, 1)], dst_ref=window,
-            send_sem=send_w.at[d - 1], recv_sem=recv_w,
-            device_id={"cond": partner(ic, d, nc)}, device_id_type=MESH,
-        )
-
-    own_window = pltpu.make_async_copy(wave.at[pl.ds(0, 1)], window, local.at[5])
-
-    @pl.when(ic == 0)
-    def _():
-        for d in range(nc - 1, 0, -1):
-            window_copy(d).start()
-        own_window.start()
-
-    def exchange(axis, position, size, d, at, src, dst, send, recv):
-        return pltpu.make_async_remote_copy(
-            src_ref=src, dst_ref=dst.at[at],
-            send_sem=send.at[d - 1], recv_sem=recv.at[d - 1],
-            device_id={axis: partner(position, d, size)}, device_id_type=MESH,
-        )
-
-    def val_copies(d, at):
-        return [
-            exchange("val", iv, nv, d, at, val, gath_v, send_v, recv_v),
-            exchange("val", iv, nv, d, at, val_energy, gath_ve, send_ve, recv_ve),
-        ]
-
-    def cond_copies(d, at):
-        return [
-            exchange("cond", ic, nc, d, at, cond, gath_c, send_c, recv_c),
-            exchange("cond", ic, nc, d, at, cond_energy, gath_ce, send_ce, recv_ce),
-        ]
-
-    for d in range(nc - 1, 0, -1):
-        for copy in cond_copies(d, ic):
-            copy.start()
-    for d in range(1, nv):
-        for copy in val_copies(d, iv):
-            copy.start()
 
     for copy in own_copies:
         copy.wait()

time: 14.4 us -> 14.4 us (level)
  no operation moved by 1% of the time
where the time goes in v3:
time: 14.4 us; the launch traced here: 14.2 us
  Pallas kernels  12.9 us (90%)
  other arithmetic  0.66 us (5%)
  between operations  0.64 us (4%)
    pallas_call x1, Pallas kernels, per_device(): pl.pallas_call(functools.partial(kernel, nv, nc, group, slots), out_shape...  12.9 us
    mul x1, other arithmetic, per_device(): return (factor * out[0:rows], factor * out[rows:2 * rows])  0.66 us

profile of v3, /device:TPU:0, one launch (start us, length us, event | category | flops | bytes accessed | tf_op | source)
XLA Modules:
  0.0 14.2 jit_solution(8311124590731715835)
XLA Ops:
  0.6 12.9 %shard_map.68 = f32[64,512]{1,0:T(8,128)S(1)} custom-call(bf16[4,768]{1,0:T(4,128)(2,1)} %val.1, bf16[8,768]{1,0:T(8,128)(2,1)} %cond.1, bf16[1,4]{1,0:T(2,128)(2,1)} %bitcast.4, bf16[1,8]{1,0:T(2,128)(2,1)} %bitcast.5, s32[4,128]{1,0:T(4,128)} %bitcast.3), custom_call_target="tpu_custom_call" | custom-call | tf_op jit(solution)/shard_map/pallas_call | solution.py:274
  13.6 0.7 %slice_multiply_fusion = (f32[32,512]{1,0:T(8,128)}, f32[32,512]{1,0:T(8,128)}) fusion(f32[64,512]{1,0:T(8,128)S(1)} %shard_map.68), kind=kLoop, calls=%fused_computation | loop fusion | flops 32768 | bytes 262144 | tf_op jit(solution)/shard_map/mul | solution.py:306

commit v4 on v3

--- a/solution.py
+++ b/solution.py
@@ -112,11 +112,14 @@
     wave_copy.start()
     for copy in own_copies:
         copy.start()
+    wave_copy.wait()
+    for copy in own_copies:
+        copy.wait()
     pl.semaphore_wait(barrier, nc - 1 + nv - 1)
 
     def window_copy(d):
         return pltpu.make_async_remote_copy(
-            src_ref=wave.at[pl.ds(0, 1)], dst_ref=window,
+            src_ref=own_wave.at[pl.ds(0, 1)], dst_ref=window,
             send_sem=send_w.at[d - 1], recv_sem=recv_w,
             device_id={"cond": partner(ic, d, nc)}, device_id_type=MESH,
         )
@@ -138,14 +141,14 @@
 
     def val_copies(d, at):
         return [
-            exchange("val", iv, nv, d, at, val, gath_v, send_v, recv_v),
-            exchange("val", iv, nv, d, at, val_energy, gath_ve, send_ve, recv_ve),
+            exchange("val", iv, nv, d, at, gath_v.at[iv], gath_v, send_v, recv_v),
+            exchange("val", iv, nv, d, at, gath_ve.at[iv], gath_ve, send_ve, recv_ve),
         ]
 
     def cond_copies(d, at):
         return [
-            exchange("cond", ic, nc, d, at, cond, gath_c, send_c, recv_c),
-            exchange("cond", ic, nc, d, at, cond_energy, gath_ce, send_ce, recv_ce),
+            exchange("cond", ic, nc, d, at, gath_c.at[ic], gath_c, send_c, recv_c),
+            exchange("cond", ic, nc, d, at, gath_ce.at[ic], gath_ce, send_ce, recv_ce),
         ]
 
     for d in range(nc - 1, 0, -1):
@@ -154,8 +157,6 @@
     for d in range(1, nv):
         for copy in val_copies(d, iv):
             copy.start()
-
-    wave_copy.wait()
 
     for block in range(own_wave.shape[0]):
         cos_x, sin_x, cos_p, sin_p = factors(own_wave[pl.ds(block, 1), :], points, 0.0)
@@ -166,8 +167,6 @@
             cos_rows[at, lanes] = (cos_x * c - sin_x * s).astype(jnp.bfloat16)
             sin_rows[at, lanes] = (sin_x * c + cos_x * s).astype(jnp.bfloat16)
 
-    for copy in own_copies:
-        copy.wait()
     for d in range(1, nv):
         for copy in val_copies(d, source(iv, d, nv)):
             copy.wait_recv()

time: 14.4 us -> 14.2 us (0.986)
    pallas_call x1, Pallas kernels: 12.9 us -> 12.8 us  [per_device(): pl.pallas_call(functools.partial(kernel, nv, nc, group, slots), out_shape...]
where the time goes in v4:
time: 14.2 us; the launch traced here: 14.1 us
  Pallas kernels  12.8 us (90%)
  other arithmetic  0.66 us (5%)
  between operations  0.64 us (5%)
    pallas_call x1, Pallas kernels, per_device(): pl.pallas_call(functools.partial(kernel, nv, nc, group, slots), out_shape...  12.8 us
    mul x1, other arithmetic, per_device(): return (factor * out[0:rows], factor * out[rows:2 * rows])  0.66 us

profile of v4, /device:TPU:0, one launch (start us, length us, event | category | flops | bytes accessed | tf_op | source)
XLA Modules:
  0.0 14.1 jit_solution(7623193935876282667)
XLA Ops:
  0.6 12.8 %shard_map.68 = f32[64,512]{1,0:T(8,128)S(1)} custom-call(bf16[4,768]{1,0:T(4,128)(2,1)} %val.1, bf16[8,768]{1,0:T(8,128)(2,1)} %cond.1, bf16[1,4]{1,0:T(2,128)(2,1)} %bitcast.4, bf16[1,8]{1,0:T(2,128)(2,1)} %bitcast.5, s32[4,128]{1,0:T(4,128)} %bitcast.3), custom_call_target="tpu_custom_call" | custom-call | tf_op jit(solution)/shard_map/pallas_call | solution.py:273
  13.4 0.7 %slice_multiply_fusion = (f32[32,512]{1,0:T(8,128)}, f32[32,512]{1,0:T(8,128)}) fusion(f32[64,512]{1,0:T(8,128)S(1)} %shard_map.68), kind=kLoop, calls=%fused_computation | loop fusion | flops 32768 | bytes 262144 | tf_op jit(solution)/shard_map/mul | solution.py:305

commit v5 on v4

--- a/solution.py
+++ b/solution.py
@@ -152,8 +152,9 @@
         ]
 
     for d in range(nc - 1, 0, -1):
-        for copy in cond_copies(d, ic):
-            copy.start()
+        cond_copies(d, ic)[1].start()
+    for d in range(nc - 1, 0, -1):
+        cond_copies(d, ic)[0].start()
     for d in range(1, nv):
         for copy in val_copies(d, iv):
             copy.start()
@@ -177,16 +178,24 @@
 
     def fill(first):
         slot = first // group % slots
-        orbitals, energies = [], []
-        for d in range(first, first + group):
-            at = source(ic, d, nc) if d else ic
+        orbitals, energies, weights = [], [], []
+        places = [source(ic, d, nc) if d else ic for d in range(first, first + group)]
+        for d, at in zip(range(first, first + group), places):
             if d:
-                for copy in cond_copies(d, at):
-                    copy.wait_recv()
-            orbitals.append(gath_c[at].astype(jnp.float32))
+                cond_copies(d, at)[1].wait_recv()
             row = jnp.broadcast_to(gath_ce[at].astype(jnp.float32), (cb, cb))
             column = jnp.sum(jnp.where(eye, row, 0.0), axis=1, keepdims=True)
             energies.append(jnp.broadcast_to(column, (cb, LANES)))
+        energies = jnp.concatenate(energies, axis=0)
+        for b in range(nv):
+            block = gath_ve[b].astype(jnp.float32)
+            for v in range(vb):
+                own = jnp.broadcast_to(block[:, v:v + 1], (1, LANES))
+                weights.append(1.0 / (energies - own))
+        for d, at in zip(range(first, first + group), places):
+            if d:
+                cond_copies(d, at)[0].wait_recv()
+            orbitals.append(gath_c[at].astype(jnp.float32))
         orbitals = jnp.concatenate(orbitals, axis=0)
 
         def one_block(b, carry):
@@ -197,25 +206,19 @@
             return carry
 
         lax.fori_loop(0, nv, one_block, 0, unroll=nv <= 4)
-        return jnp.concatenate(energies, axis=0)
-
-    def use(first, energies):
+        return jnp.concatenate(weights, axis=0)
+
+    def use(first, weights):
         slot = first // group % slots
-        weights = []
-        for b in range(nv):
-            block = gath_ve[b].astype(jnp.float32)
-            for v in range(vb):
-                own = jnp.broadcast_to(block[:, v:v + 1], (1, LANES))
-                weights.append(1.0 / (energies - own))
-        weighted = dot(dens[slot], window_table[...]) * jnp.concatenate(weights, axis=0)
+        weighted = dot(dens[slot], window_table[...]) * weights
         update = dot(split(jnp.transpose(weighted)[0:2 * rows]), dens[slot])
         update = update[0:2 * rows] + update[2 * rows:4 * rows]
         totals[...] = update if first == 0 else totals[...] + update
 
     ahead = min(2, slots, nc // group)
-    energies = {}
+    weights = {}
     for step in range(ahead):
-        energies[step] = fill(step * group)
+        weights[step] = fill(step * group)
 
     @pl.when(ic == 0)
     def _():
@@ -237,8 +240,8 @@
 
     for step in range(nc // group):
         if step >= ahead:
-            energies[step] = fill(step * group)
-        use(step * group, energies.pop(step))
+            weights[step] = fill(step * group)
+        use(step * group, weights.pop(step))
 
     cos_total = totals[0:rows, :]
     sin_total = totals[rows:2 * rows, :]

time: 14.2 us -> 14.7 us (1.035)
  Pallas kernels: 12.8 us -> 13.3 us
    pallas_call x1, Pallas kernels: 12.8 us -> 13.3 us  [per_device(): pl.pallas_call(functools.partial(kernel, nv, nc, group, slots), out_shape...]
where the time goes in v5:
time: 14.7 us; the launch traced here: 14.6 us
  Pallas kernels  13.3 us (90%)
  other arithmetic  0.66 us (4%)
  between operations  0.64 us (4%)
    pallas_call x1, Pallas kernels, per_device(): pl.pallas_call(functools.partial(kernel, nv, nc, group, slots), out_shape...  13.3 us
    mul x1, other arithmetic, per_device(): return (factor * out[0:rows], factor * out[rows:2 * rows])  0.66 us

profile of v5, /device:TPU:0, one launch (start us, length us, event | category | flops | bytes accessed | tf_op | source)
XLA Modules:
  0.0 14.6 jit_solution(8301564493895974522)
XLA Ops:
  0.6 13.3 %shard_map.68 = f32[64,512]{1,0:T(8,128)S(1)} custom-call(bf16[4,768]{1,0:T(4,128)(2,1)} %val.1, bf16[8,768]{1,0:T(8,128)(2,1)} %cond.1, bf16[1,4]{1,0:T(2,128)(2,1)} %bitcast.4, bf16[1,8]{1,0:T(2,128)(2,1)} %bitcast.5, s32[4,128]{1,0:T(4,128)} %bitcast.3), custom_call_target="tpu_custom_call" | custom-call | tf_op jit(solution)/shard_map/pallas_call | solution.py:276
  13.9 0.7 %slice_multiply_fusion = (f32[32,512]{1,0:T(8,128)}, f32[32,512]{1,0:T(8,128)}) fusion(f32[64,512]{1,0:T(8,128)S(1)} %shard_map.68), kind=kLoop, calls=%fused_computation | loop fusion | flops 32768 | bytes 262144 | tf_op jit(solution)/shard_map/mul | solution.py:308
